TPU v7x, 32 devices: a whole 2x2x4 slice. The times are simulated.
32 devices in a mesh: section: 2 (over x), dp: 4 (over z), fsdp: 4 (over y, core).
Axes of the slice: x: 2, y: 2, z: 4, core: 2. Of those that a mesh axis runs over, the one named last changes fastest.
Arguments:
- inputs: float32 [32, 128, 1536], P(('dp', 'fsdp')), may hold values from -6 to 6
- cotangent: float32 [32, 128, 1536], P(('dp', 'fsdp')), may hold values from -6 to 6
- lengths: int32 [32], P(('dp', 'fsdp')), may hold values from 1 to 128, 2560 in all
- norm_gain: float32 [2, 1536], P('section'), may hold values from 0.5 to 1.5
- in_weight: bfloat16 [2, 1536, 6400], P('section', 'fsdp'), may hold values from -0.15625 to 0.15625
- dt_weight: bfloat16 [2, 1536, 48], P('section', 'fsdp'), may hold values from -0.15625 to 0.15625
- conv_weight: float32 [2, 4, 3328], P('section'), may hold values from -3 to 3
- conv_bias: float32 [2, 3328], P('section'), may hold values from -0.5 to 0.5
- dt_bias: float32 [2, 48], P('section'), may hold values from -4 to -1
- decay_log: float32 [2, 48], P('section'), may hold values from -4.6 to 0
- skip_gain: float32 [2, 48], P('section'), may hold values from 0.5 to 1.5
- gate_gain: float32 [2, 3072], P('section'), may hold values from 0.5 to 1.5
- out_weight: bfloat16 [2, 3072, 1536], P('section', 'fsdp'), may hold values from -0.109375 to 0.109375
Outputs:
- layer_outputs: float32 [2, 32, 128, 1536], P('section', ('dp', 'fsdp'))
- input_grads: float32 [2, 32, 128, 1536], P('section', ('dp', 'fsdp'))
- grad_norm_gain: float32 [2, 1536], P('section')
- grad_in_weight: float32 [2, 1536, 6400], P('section', 'fsdp')
- grad_dt_weight: float32 [2, 1536, 48], P('section', 'fsdp')
- grad_conv_weight: float32 [2, 4, 3328], P('section')
- grad_conv_bias: float32 [2, 3328], P('section')
- grad_dt_bias: float32 [2, 48], P('section')
- grad_decay_log: float32 [2, 48], P('section')
- grad_skip_gain: float32 [2, 48], P('section')
- grad_gate_gain: float32 [2, 3072], P('section')
- grad_out_weight: float32 [2, 3072, 1536], P('section', 'fsdp')
Inputs may be any that keep to these rules, and one draw needn't show every extreme that they name: `lengths`: positions from a sequence's length on are padding.
All inputs are finite; a program needn't handle non-finite values. No bound on the sum of `lengths` on one device may be relied on, other than what follows from the above.
Results may differ from a plain program's by a relative error of at most 0.011.
Values may be sent and summed in bfloat16 or wider, within the bound.
No kernel may reach another device: no remote copies, remote signals or barrier semaphores. Data moves between devices by JAX's collectives and lax.ppermute only.
A program may use at most 448 MiB of HBM per device.

v0:
```python
import jax
import jax.numpy as jnp
from jax import lax
from jax.sharding import PartitionSpec as P

INNER = 3072
HEADS = 48
HEAD_DIM = 64
STATE = 128
BLOCK = 64
CONV = 4
BUCKET = 128
MICRO = 2
epsilon = 1e-05
highest = lax.Precision.HIGHEST


def passed_along(block, axis, distance):
    devices = range(lax.axis_size(axis))
    route = [(i - distance, i) for i in devices if i - distance in devices]
    return lax.ppermute(block, axis, route)


def front_norm(residual, norm_gain):
    inverse = lax.rsqrt(jnp.mean(residual * residual, axis=-1, keepdims=True) + epsilon)
    return residual * inverse * norm_gain


def state_space(values, step_sizes, log_decay, inputs_b, outputs_c, skip_gain):
    seq_count, length = (values.shape[0], values.shape[1])
    blocks = length // BLOCK
    values_k = values.reshape(seq_count, blocks, BLOCK, HEADS, HEAD_DIM)
    steps_k = step_sizes.reshape(seq_count, blocks, BLOCK, HEADS)
    totals = jnp.cumsum(log_decay.reshape(seq_count, blocks, BLOCK, HEADS), axis=2)
    in_k = inputs_b.reshape(seq_count, blocks, BLOCK, STATE)
    out_k = outputs_c.reshape(seq_count, blocks, BLOCK, STATE)
    causal = (
        jnp.arange(BLOCK, dtype=jnp.int32)[:, None] >= jnp.arange(BLOCK, dtype=jnp.int32)[None, :]
    )[None, None, :, :, None]
    spread = totals[:, :, :, None, :] - totals[:, :, None, :, :]
    kernel = jnp.where(causal, jnp.exp(jnp.where(causal, spread, 0.0)), 0.0)
    inner_cb = jnp.einsum("skin,skjn->skij", out_k, in_k, precision=highest)
    weighted = inner_cb[..., None] * kernel * steps_k[:, :, None, :, :]
    local_part = jnp.einsum("skijh,skjhp->skihp", weighted, values_k, precision=highest)
    to_end = jnp.exp(totals[:, :, -1:, :] - totals) * steps_k
    scaled_values = values_k * to_end[..., None]
    block_states = jnp.einsum("skjhp,skjn->skhpn", scaled_values, in_k, precision=highest)
    carried = jnp.zeros((seq_count, HEADS, HEAD_DIM, STATE), jnp.float32)
    entering = []
    for block_index in range(blocks):
        entering.append(carried)
        carried = (
            jnp.exp(totals[:, block_index, -1, :])[:, :, None, None] * carried
            + block_states[:, block_index]
        )
    entering_all = jnp.stack(entering, axis=1)
    carried_part = (
        jnp.einsum("skin,skhpn->skihp", out_k, entering_all, precision=highest)
        * jnp.exp(totals)[..., None]
    )
    result = (local_part + carried_part).reshape(seq_count, length, HEADS, HEAD_DIM)
    return result + skip_gain[:, None] * values


def mixer_core(projected, dt_raw, conv_weight, conv_bias, dt_bias, decay_log, skip_gain, gate_gain):
    row_count = projected.shape[0]
    seq_count = row_count // BUCKET
    shaped = projected.reshape(seq_count, BUCKET, projected.shape[1])
    gate_part = shaped[:, :, :INNER]
    conv_input = shaped[:, :, INNER:]
    padded = jnp.pad(conv_input, ((0, 0), (CONV - 1, 0), (0, 0)))
    convolved = conv_bias + conv_weight[0] * padded[:, 0:BUCKET]
    for offset in range(1, CONV):
        convolved = convolved + conv_weight[offset] * padded[:, offset : offset + BUCKET]
    activated = jax.nn.silu(convolved)
    values = activated[:, :, :INNER].reshape(seq_count, BUCKET, HEADS, HEAD_DIM)
    inputs_b = activated[:, :, INNER : INNER + STATE]
    outputs_c = activated[:, :, INNER + STATE :]
    step_sizes = jax.nn.softplus(dt_raw.reshape(seq_count, BUCKET, HEADS) + dt_bias)
    log_decay = -jnp.exp(decay_log) * step_sizes
    scanned = state_space(values, step_sizes, log_decay, inputs_b, outputs_c, skip_gain).reshape(
        seq_count, BUCKET, INNER
    )
    gated_out = scanned * jax.nn.silu(gate_part)
    inverse = lax.rsqrt(jnp.mean(gated_out * gated_out, axis=-1, keepdims=True) + epsilon)
    return (gated_out * inverse * gate_gain).reshape(row_count, INNER)


def layer_forward(residual, params):
    norm_gain, in_weight, dt_weight, small_params, out_weight = params
    normed = front_norm(residual, norm_gain).astype(jnp.bfloat16)
    projected = jnp.dot(normed, in_weight, preferred_element_type=jnp.float32)
    dt_raw = jnp.dot(normed, dt_weight, preferred_element_type=jnp.float32)
    mixed_out = mixer_core(projected, dt_raw, *small_params).astype(jnp.bfloat16)
    output = residual + jnp.dot(mixed_out, out_weight, preferred_element_type=jnp.float32)
    return (output, (normed, projected, dt_raw, mixed_out))


def contract_rows(left, right):
    return lax.dot_general(
        left, right, (((0,), (0,)), ((), ())), preferred_element_type=jnp.float32
    )


def contract_cols(left, right):
    return lax.dot_general(
        left, right, (((1,), (1,)), ((), ())), preferred_element_type=jnp.float32
    )


def column_term(columns, grads):
    return contract_rows(columns, grads)


def reorder(columns, data_groups, owners):
    row_count, total_cols = columns.shape
    shaped = columns.reshape(row_count, owners, data_groups, total_cols // (owners * data_groups))
    return shaped.transpose(0, 2, 1, 3).reshape(row_count, total_cols)


def per_device(
    inputs,
    cotangent,
    lengths,
    norm_gain,
    in_weight,
    dt_weight,
    conv_weight,
    conv_bias,
    dt_bias,
    decay_log,
    skip_gain,
    gate_gain,
    out_weight,
):
    first_section = lax.axis_index("section") == 0
    full_in, full_dt, full_out = (
        lax.all_gather(in_weight[0], "fsdp", axis=0, tiled=True),
        lax.all_gather(dt_weight[0], "fsdp", axis=0, tiled=True),
        lax.all_gather(out_weight[0], "fsdp", axis=0, tiled=True),
    )
    small_params = (
        conv_weight[0],
        conv_bias[0],
        dt_bias[0],
        decay_log[0],
        skip_gain[0],
        gate_gain[0],
    )
    own_gain = norm_gain[0]
    params = (own_gain, full_in, full_dt, small_params, full_out)
    per_micro = inputs.shape[0] // MICRO
    row_count = per_micro * BUCKET
    model_width = inputs.shape[2]
    proj_cols = full_in.shape[1]
    data_groups = lax.axis_size("dp")
    owners = lax.axis_size("fsdp")
    positions = jnp.arange(BUCKET, dtype=jnp.int32)
    empty_rows = jnp.zeros((row_count, model_width), jnp.float32)

    def micro_rows(source, micro_index):
        return source[micro_index * per_micro : (micro_index + 1) * per_micro].reshape(
            row_count, model_width
        )

    def arrange(columns):
        return reorder(columns, data_groups, owners)

    layer_inputs = []
    results = []
    kept_all = []
    for section_tick in range(MICRO + 1):
        if section_tick > 0:
            arrived = passed_along(results[-1], "section", 1)
        else:
            arrived = empty_rows
        own_rows = micro_rows(inputs, section_tick) if section_tick < MICRO else empty_rows
        residual = jnp.where(first_section, own_rows, arrived)
        output, kept_values = layer_forward(residual, params)
        layer_inputs.append(residual)
        results.append(output)
        kept_all.append(kept_values)
    small_acc = (jnp.zeros(own_gain.shape, jnp.float32),) + tuple(
        (jnp.zeros(a.shape, jnp.float32) for a in small_params)
    )
    total_in = None
    total_out = None
    grads_back = []
    for section_tick in range(MICRO + 1):
        if section_tick > 0:
            returned = passed_along(grads_back[-1], "section", -1)
        else:
            returned = empty_rows
        if section_tick < MICRO:
            own_lengths = lengths[section_tick * per_micro : (section_tick + 1) * per_micro]
            live_rows = (positions[None, :] < own_lengths[:, None]).astype(jnp.float32)
            top_grad = micro_rows(cotangent, section_tick) * live_rows.reshape(row_count, 1)
        else:
            top_grad = empty_rows
        later_tick = min(section_tick + 1, MICRO)
        earlier = max(section_tick - 1, 0)
        grad_output = jnp.where(first_section, returned, top_grad)
        residual = jnp.where(first_section, layer_inputs[earlier], layer_inputs[later_tick])
        normed, projected, dt_raw, mixed_out = jax.tree.map(
            lambda a, b: jnp.where(first_section, a, b), kept_all[earlier], kept_all[later_tick]
        )
        grad_rounded = grad_output.astype(jnp.bfloat16)
        grad_mixed = contract_cols(grad_rounded, full_out)
        _, pull_mixer = jax.vjp(mixer_core, projected, dt_raw, *small_params)
        pulled = pull_mixer(grad_mixed)
        grad_proj = pulled[0].astype(jnp.bfloat16)
        grad_dt = pulled[1].astype(jnp.bfloat16)
        grad_cat = jnp.concatenate([grad_proj, grad_dt], axis=1)
        grad_normed = contract_cols(grad_proj, full_in) + contract_cols(grad_dt, full_dt)
        _, pull_front = jax.vjp(front_norm, residual, own_gain)
        grad_residual, grad_gain = pull_front(grad_normed)
        grads_back.append(grad_output + grad_residual)
        small_acc = tuple((a + b for a, b in zip(small_acc, (grad_gain,) + tuple(pulled[2:]))))
        normed_cols = arrange(normed)
        mixed_cols = arrange(mixed_out)
        part_in = lax.psum_scatter(
            column_term(normed_cols, grad_cat), ("dp", "fsdp"), scatter_dimension=0, tiled=True
        )
        part_out = lax.psum_scatter(
            column_term(mixed_cols, grad_rounded), ("dp", "fsdp"), scatter_dimension=0, tiled=True
        )
        total_in = part_in if total_in is None else total_in + part_in
        total_out = part_out if total_out is None else total_out + part_out
    owned_in, owned_out = (
        lax.all_gather(total_in, "dp", axis=0, tiled=True),
        lax.all_gather(total_out, "dp", axis=0, tiled=True),
    )
    small_total = lax.psum(small_acc, ("dp", "fsdp"))
    layer_out = jnp.concatenate(
        [
            jnp.where(first_section, results[m], results[m + 1]).reshape(
                per_micro, BUCKET, model_width
            )
            for m in range(MICRO)
        ],
        axis=0,
    )
    input_grad = jnp.concatenate(
        [
            jnp.where(first_section, grads_back[m + 1], grads_back[m]).reshape(
                per_micro, BUCKET, model_width
            )
            for m in range(MICRO)
        ],
        axis=0,
    )
    grad_in_part = owned_in[:, :proj_cols]
    grad_dt_part = owned_in[:, proj_cols:]
    return (
        layer_out[None],
        input_grad[None],
        small_total[0][None],
        grad_in_part[None],
        grad_dt_part[None],
        small_total[1][None],
        small_total[2][None],
        small_total[3][None],
        small_total[4][None],
        small_total[5][None],
        small_total[6][None],
        owned_out[None],
    )


def solution(mesh):
    in_specs = (
        P(("dp", "fsdp"), None, None),
        P(("dp", "fsdp"), None, None),
        P(("dp", "fsdp")),
        P("section", None),
        P("section", "fsdp", None),
        P("section", "fsdp", None),
        P("section", None, None),
        P("section", None),
        P("section", None),
        P("section", None),
        P("section", None),
        P("section", None),
        P("section", "fsdp", None),
    )
    out_specs = (
        P("section", ("dp", "fsdp"), None, None),
        P("section", ("dp", "fsdp"), None, None),
        P("section", None),
        P("section", "fsdp", None),
        P("section", "fsdp", None),
        P("section", None, None),
        P("section", None),
        P("section", None),
        P("section", None),
        P("section", None),
        P("section", None),
        P("section", "fsdp", None),
    )
    return jax.shard_map(
        per_device, mesh=mesh, in_specs=in_specs, out_specs=out_specs, check_vma=False
    )
```

profile of v0, /device:TPU:0, one launch (start us, length us, event | category | flops | bytes accessed | tf_op | source)
XLA Modules:
  0.0 1780.0 jit_solution(17367377292099813090)
XLA Ops:
  8.9 6.6 all-gather.1
  19.5 117.1 %all-gather.12.cloned.1.call-done = bf16[1,1536,6400]{2,1,0:T(8,128)(2,1)} async-done(((bf16[1,384,6400]{2,1,0:T(8,128)(2,1)}), bf16[1,1536,6400]{2,1,0:T(8,128)(2,1)}) %all-gather.12.cloned.1.call-update) | async-done | bytes 19660816 | tf_op jit(solution)/shard_map/all_gather | solution.py:138
  136.7 8.1 fusion.10
  163.3 6.0 fusion.113
  184.4 18.1 %all-gather.14.cloned.1.call-done = bf16[1,3072,1536]{2,1,0:T(8,128)(2,1)} async-done(((bf16[1,768,1536]{2,1,0:T(8,128)(2,1)}), bf16[1,3072,1536]{2,1,0:T(8,128)(2,1)}) %all-gather.14.cloned.1.call-update) | async-done | bytes 9437200 | tf_op jit(solution)/shard_map/all_gather | solution.py:140
  214.1 14.1 collective-permute-done
  231.9 8.2 fusion.8
  270.1 6.0 fusion.103
  310.2 8.7 fusion.396
  321.8 8.4 fusion.6
  340.5 5.9 fusion.204
  358.7 6.9 fusion.165
  370.8 7.8 bitcast_add_fusion.5
  388.8 9.2 fusion.241
  421.5 6.0 fusion.93
  439.4 7.5 multiply_reduce_fusion.20
  457.0 5.5 fusion.168
  464.4 10.0 fusion.225
  498.7 7.4 fusion.329
  517.2 6.9 fusion.171
  530.0 8.0 bitcast_add_fusion.3
  542.8 6.6 bitcast_add_fusion.4
  571.6 14.4 fusion.4
  611.8 7.9 fusion.240
  634.9 5.5 fusion.174
  643.2 11.1 fusion.227
  681.2 8.2 fusion.344
  694.0 6.8 fusion.177
  707.1 7.6 bitcast_add_fusion.1
  721.7 7.4 bitcast_add_fusion.2
  736.7 6.2 fusion.354
  754.3 14.3 fusion.2
  784.1 8.0 fusion.404
  792.6 21.3 %add_add_fusion.1 = f32[3072,1536]{1,0:T(8,128)} fusion(f32[3072,1536]{1,0:T(8,128)} %fusion.396, f32[3072,1536]{1,0:T(8,128)} %fusion.404, bf16[128,3072]{0,1:T(8,128)(2,1)} %bitcast.975, f32[128,1536]{1,0:T(8,128)} %collective-permute-done.3, pred[]{:T(512)S(6)} %eq.9), kind=kOutput, calls=%fused_computation.13 | convolution fusion | flops 1217593344 | bytes 58195968 | tf_op jit(solution)/shard_map/dot_general | solution.py:100
  834.1 19.9 %fusion.213 = f32[1536,6448]{1,0:T(8,128)} fusion(bf16[128,1536]{0,1:T(8,128)(2,1)S(1)} %bitcast.1029, bf16[128,48]{1,0:T(8,128)(2,1)} %bitcast.1059, bf16[128,6400]{1,0:T(8,128)(2,1)} %copy-done.45), kind=kOutput, calls=%fused_computation.278 | convolution fusion | flops 2538758144 | bytes 41660416 | tf_op jit(solution)/shard_map/dot_general | solution.py:100
  854.0 17.7 fusion.217
  871.8 5.7 fusion.239
  908.2 6.0 bitcast_add_fusion
  921.3 10.7 fusion.229
  948.3 7.7 fusion.359
  967.9 40.4 %add_add_fusion = f32[1536,6448]{1,0:T(8,128)} fusion(f32[1536,6448]{1,0:T(8,128)} %fusion.213, f32[1536,6448]{1,0:T(8,128)} %fusion.217, bf16[128,1536]{0,1:T(8,128)(2,1)S(1)} %bitcast.994, bf16[128,48]{1,0:T(8,128)(2,1)S(1)} %bitcast.1058, bf16[128,6400]{1,0:T(8,128)(2,1)S(1)} %fusion.232), kind=kOutput, calls=%fused_computation | convolution fusion | flops 2558566400 | bytes 120893440 | tf_op jit(solution)/shard_map/dot_general | solution.py:100
  1009.5 390.6 %reduce-scatter.3.cloned.1.call-done = f32[96,6448]{1,0:T(8,128)} async-done(((f32[1536,6448]{1,0:T(8,128)}), f32[96,6448]{1,0:T(8,128)}) %reduce-scatter.3.cloned.1.call-update) | async-done | bytes 2476048 | tf_op jit(solution)/shard_map/reduce_scatter | solution.py:221
  1404.5 5.6 fusion.162
  1414.6 10.4 fusion
  1433.2 56.9 %all-gather.10.cloned.1.call-done = f32[768,1536]{1,0:T(8,128)} async-done(((f32[192,1536]{1,0:T(8,128)}), f32[768,1536]{1,0:T(8,128)}) %all-gather.10.cloned.1.call-update) | async-done | bytes 4718608 | tf_op jit(solution)/shard_map/all_gather | solution.py:231
  1490.0 176.3 %all-gather.8.cloned.1.call-done = f32[384,6448]{1,0:T(8,128)} async-done(((f32[96,6448]{1,0:T(8,128)}), f32[384,6448]{1,0:T(8,128)}) %all-gather.8.cloned.1.call-update) | async-done | bytes 9904144 | tf_op jit(solution)/shard_map/all_gather | solution.py:230
  1666.3 8.3 slice_bitcast_fusion
  1676.3 83.1 %all-reduce.63.cloned.1.call-done = (f32[1,1536]{1,0:T(1,128)}, f32[1,4,3328]{2,1,0:T(4,128)}, f32[1,3328]{1,0:T(1,128)}, f32[1,48]{1,0:T(1,128)}, f32[1,48]{1,0...) async-done(((f32[1,1536]{1,0:T(1,128)}, f32[1,4,3328]{2,1,0:T(4,128)}, f32[1,3328]{1,0:T(1,128)}, f32[1,48]{1,0:T(1,128)}, f32[1,48]{1,0:T(1,128)}, ...) | async-done | bytes 85584 | tf_op jit(solution)/shard_map/psum | solution.py:233
  (925 shorter events, 515.1 us)
Async XLA Ops:
  7.2 129.5 %all-gather.12.cloned.1.call-start = ((), (), s32[]{:S(2)}) async-start(), calls=%async_computation.4 | async-start | bytes 24576000 | tf_op jit(solution)/shard_map/all_gather | solution.py:138
  8.0 194.5 %all-gather.14.cloned.1.call-start = ((), (), s32[]{:S(2)}) async-start(), calls=%async_computation.5 | async-start | bytes 11796480 | tf_op jit(solution)/shard_map/all_gather | solution.py:140
  8.7 1000.7 %reduce-scatter.5.cloned.1.call-start = ((), (), s32[]{:S(2)}) async-start(), calls=%async_computation.7 | async-start | bytes 20054016 | tf_op jit(solution)/shard_map/reduce_scatter | solution.py:224
  8.8 221.1 %copy-start.142 = (f32[1536]{0:T(1024)}, f32[1536]{0:T(1024)S(1)}, u32[]{:S(2)}) copy-start(f32[1536]{0:T(1024)S(1)} %reduce.80) | copy-start | bytes 18436
  8.9 137.6 %copy-start.211 = (f32[3328]{0:T(1024)}, f32[3328]{0:T(1024)S(1)}, u32[]{:S(2)}) copy-start(f32[3328]{0:T(1024)S(1)} %reduce.78) | copy-start | bytes 39940
  15.5 753.1 %copy-start.78 = (bf16[1,1536,48]{1,2,0:T(8,128)(2,1)}, bf16[1,1536,48]{1,2,0:T(8,128)(2,1)S(1)}, u32[]{:S(2)}) copy-start(bf16[1,1536,48]{1,2,0:T(8,128)(2,1)S(1)} %all-gather.1) | copy-start | bytes 442372
  15.7 129.1 %copy-start.261 = (f32[128]{0:T(128)}, f32[128]{0:T(128)S(1)}, u32[]{:S(2)}) copy-start(f32[128]{0:T(128)S(1)} %add_rsqrt_fusion.5) | copy-start | bytes 1540
  15.7 230.8 %copy-start.253 = (f32[48]{0:T(128)}, f32[48]{0:T(128)S(1)}, u32[]{:S(2)}) copy-start(f32[48]{0:T(128)S(1)} %bitcast_negate_fusion) | copy-start | bytes 580
  16.2 230.4 %copy-start.140 = (f32[128,48]{1,0:T(8,128)}, f32[128,48]{1,0:T(8,128)S(1)}, u32[]{:S(2)}) copy-start(f32[128,48]{1,0:T(8,128)S(1)} %get-tuple-element.253) | copy-start | bytes 73732
  19.3 268.4 %copy-start.135 = (f32[3072]{0:T(1024)}, f32[3072]{0:T(1024)S(1)}, u32[]{:S(2)}) copy-start(f32[3072]{0:T(1024)S(1)} %mul.1954) | copy-start | bytes 36868
  19.3 249.1 %copy-start.194 = (pred[64,64]{1,0:T(8,128)(4,1)}, pred[64,64]{1,0:T(8,128)(4,1)S(1)}, u32[]{:S(2)}) copy-start(pred[64,64]{1,0:T(8,128)(4,1)S(1)} %iota_compare_fusion) | copy-start | bytes 12292
  19.5 220.8 %copy-start.147 = (f32[3328]{0:T(1024)}, f32[3328]{0:T(1024)S(1)}, u32[]{:S(2)}) copy-start(f32[3328]{0:T(1024)S(1)} %get-tuple-element.111) | copy-start | bytes 39940
  19.5 220.8 %copy-start.152 = (f32[3328]{0:T(1024)}, f32[3328]{0:T(1024)S(1)}, u32[]{:S(2)}) copy-start(f32[3328]{0:T(1024)S(1)} %get-tuple-element.112) | copy-start | bytes 39940
  19.5 220.8 %copy-start.157 = (f32[3328]{0:T(1024)}, f32[3328]{0:T(1024)S(1)}, u32[]{:S(2)}) copy-start(f32[3328]{0:T(1024)S(1)} %get-tuple-element.113) | copy-start | bytes 39940
  19.5 220.8 %copy-start.162 = (f32[3328]{0:T(1024)}, f32[3328]{0:T(1024)S(1)}, u32[]{:S(2)}) copy-start(f32[3328]{0:T(1024)S(1)} %get-tuple-element.114) | copy-start | bytes 39940
  181.3 21.2 %copy-start.111 = (f32[1,3072]{1,0:T(1,128)S(1)}, f32[1,3072]{1,0:T(1,128)}, u32[]{:S(2)}) copy-start(f32[1,3072]{1,0:T(1,128)} %param.25) | copy-start | bytes 36868
  184.4 106.4 %copy-start.7 = (f32[1,128,3072]{2,1,0:T(8,128)}, f32[1,128,3072]{2,1,0:T(8,128)S(1)}, u32[]{:S(2)}) copy-start(f32[1,128,3072]{2,1,0:T(8,128)S(1)} %get-tuple-element.181) | copy-start | bytes 4718596
  184.4 23.2 %copy-start.257 = (f32[128]{0:T(128)}, f32[128]{0:T(128)S(1)}, u32[]{:S(2)}) copy-start(f32[128]{0:T(128)S(1)} %add_rsqrt_fusion.4) | copy-start | bytes 1540
  207.6 22.1 %copy-start.103 = (f32[128,1536]{1,0:T(8,128)}, f32[128,1536]{1,0:T(8,128)S(1)}, u32[]{:S(2)}) copy-start(f32[128,1536]{1,0:T(8,128)S(1)} %fusion.150) | copy-start | bytes 2359300
  207.6 20.6 %collective-permute-start = (f32[128,1536]{1,0:T(8,128)S(1)}, f32[128,1536]{1,0:T(8,128)S(1)}, u32[]{:S(2)}, u32[]{:S(2)}) collective-permute-start(f32[128,1536]{1,0:T(8,128)S(1)} %fusion.150), channel_id=1, source_target_pairs={{0,16},{1,17},{2,18},{3,19},{4,20},{5,21},{6,22},{7,23},{8,24},{9,... | collective-permute-start | bytes 2359304 | tf_op jit(solution)/shard_map/ppermute | solution.py:21
  214.1 15.8 copy-start.262
  231.9 14.7 copy-start.128
  297.5 21.3 %collective-permute-start.1 = (f32[128,1536]{1,0:T(8,128)S(1)}, f32[128,1536]{1,0:T(8,128)S(1)}, u32[]{:S(2)}, u32[]{:S(2)}) collective-permute-start(f32[128,1536]{1,0:T(8,128)S(1)} %fusion.153), channel_id=1, source_target_pairs={{0,16},{1,17},{2,18},{3,19},{4,20},{5,21},{6,22},{7,23},{8,24},{9,... | collective-permute-start | bytes 2359304 | tf_op jit(solution)/shard_map/ppermute | solution.py:21
  321.8 28.3 %copy-start.98 = (bf16[128,1536]{1,0:T(8,128)(2,1)}, bf16[128,1536]{1,0:T(8,128)(2,1)S(1)}, u32[]{:S(2)}) copy-start(bf16[128,1536]{1,0:T(8,128)(2,1)S(1)} %get-tuple-element.127) | copy-start | bytes 1179652
  348.8 108.2 %copy-start.118 = (f32[1,128,128]{2,1,0:T(8,128)}, f32[1,128,128]{2,1,0:T(8,128)S(1)}, u32[]{:S(2)}) copy-start(f32[1,128,128]{2,1,0:T(8,128)S(1)} %get-tuple-element.213) | copy-start | bytes 196612
  354.2 109.9 %copy-start.2 = (f32[2,64,48,64]{3,2,1,0:T(8,128)}, f32[2,64,48,64]{3,2,1,0:T(8,128)S(1)}, u32[]{:S(2)}) copy-start(f32[2,64,48,64]{3,2,1,0:T(8,128)S(1)} %reshape.2331) | copy-start | bytes 4718596
  509.5 82.0 %copy-start.112 = (f32[1,128,128]{2,1,0:T(8,128)}, f32[1,128,128]{2,1,0:T(8,128)S(1)}, u32[]{:S(2)}) copy-start(f32[1,128,128]{2,1,0:T(8,128)S(1)} %get-tuple-element.201) | copy-start | bytes 196612
  511.7 16.1 copy-start
  571.5 14.4 copy-start.45
  571.5 14.4 copy-start.82
  571.6 14.4 copy-start.144
  571.6 14.4 copy-start.201
  571.6 14.4 copy-start.276
  589.5 20.9 %collective-permute-start.2 = (f32[128,1536]{1,0:T(8,128)}, f32[128,1536]{1,0:T(8,128)}, u32[]{:S(2)}, u32[]{:S(2)}) collective-permute-start(f32[128,1536]{1,0:T(8,128)} %fusion.374), channel_id=1, source_target_pairs={{16,0},{17,1},{18,2},{19,3},{20,4},{21,5},{22,6},{23,7},{24,8},{25... | collective-permute-start | bytes 2359304 | tf_op jit(solution)/shard_map/ppermute | solution.py:21
  675.8 14.3 copy-start.108
  676.8 17.1 copy-start.106
  754.3 14.3 copy-start.265
  772.7 19.9 %collective-permute-start.3 = (f32[128,1536]{1,0:T(8,128)}, f32[128,1536]{1,0:T(8,128)}, u32[]{:S(2)}, u32[]{:S(2)}) collective-permute-start(f32[128,1536]{1,0:T(8,128)} %get-tuple-element.146), channel_id=1, source_target_pairs={{16,0},{17,1},{18,2},{19,3},{20,4},{21,5},{22,6},{23,7},{24,8},{25... | collective-permute-start | bytes 2359304 | tf_op jit(solution)/shard_map/ppermute | solution.py:21
  813.9 586.2 %reduce-scatter.3.cloned.1.call-start = ((), (), s32[]{:S(2)}) async-start(), calls=%async_computation.6 | async-start | bytes 42614784 | tf_op jit(solution)/shard_map/reduce_scatter | solution.py:221
  834.1 19.9 %copy-start.280 = (f32[128]{0:T(128)S(1)}, f32[128]{0:T(128)}, u32[]{:S(2)}) copy-start(f32[128]{0:T(128)} %get-tuple-element.149) | copy-start | bytes 1540
  834.1 19.9 %copy-start.203 = (bf16[1,128,48]{2,1,0:T(8,128)(2,1)S(1)}, bf16[1,128,48]{2,1,0:T(8,128)(2,1)}, u32[]{:S(2)}) copy-start(bf16[1,128,48]{2,1,0:T(8,128)(2,1)} %get-tuple-element.137) | copy-start | bytes 36868
  834.1 37.6 %slice-start = ((s8[9437184]{0:T(1024)(128)(4,1)}), s8[4194304]{0:T(1024)(128)(4,1)S(1)}, s32[]{:S(2)}) async-start(s8[9437184]{0:T(1024)(128)(4,1)} %bitcast.961), calls=%async_computation.9 | async-start | bytes 8388608
  834.1 37.6 %slice-start.1 = ((s8[9437184]{0:T(1024)(128)(4,1)}), s8[4194304]{0:T(1024)(128)(4,1)S(1)}, s32[]{:S(2)}) async-start(s8[9437184]{0:T(1024)(128)(4,1)} %bitcast.961), calls=%async_computation.10 | async-start | bytes 8388608
  854.0 17.7 slice-start.2
  1008.4 481.6 %all-gather.10.cloned.1.call-start = ((), (), s32[]{:S(2)}) async-start(), calls=%async_computation.3 | async-start | bytes 5898240 | tf_op jit(solution)/shard_map/all_gather | solution.py:231
  1009.4 390.9 %copy-start.81 = (f32[128,1536]{1,0:T(8,128)S(1)}, f32[128,1536]{1,0:T(8,128)}, u32[]{:S(2)}) copy-start(f32[128,1536]{1,0:T(8,128)} %copy-done.80) | copy-start | bytes 2359300
  1009.5 656.8 %all-gather.8.cloned.1.call-start = ((), (), s32[]{:S(2)}) async-start(), calls=%async_computation.2 | async-start | bytes 12533760 | tf_op jit(solution)/shard_map/all_gather | solution.py:230
  1400.2 359.1 %all-reduce.63.cloned.1.call-start = ((), (), s32[]{:S(2)}) async-start(), calls=%async_computation.8 | async-start | bytes 173056 | tf_op jit(solution)/shard_map/psum | solution.py:233
  (260 other events, 1109.6 us)
Sparse Core Ops, SparseCore 0:
  9.6 127.0 all-gather.11
  138.2 64.2 all-gather.13
  814.1 195.3 reduce-scatter.4
  1013.6 386.4 reduce-scatter.2
  1401.6 88.4 all-gather.9
  1491.4 174.7 all-gather.7
  1671.8 87.5 all-reduce.62
where the time goes:
time: 1790 us; the launch traced here: 1780 us
  waiting for transfers between devices  865 us (48%)
  matrix products  454 us (25%)
  local copies, waits for them, and re-layouts  295 us (16%)
  other arithmetic  132 us (7%)
    reduce_scatter x1, waiting for transfers between devices, per_device(): lax.psum_scatter(column_term(normed_cols, grad_cat), ('dp', 'fsdp'), scat...  391 us
    all_gather x1, waiting for transfers between devices, per_device(): lax.all_gather(total_in, 'dp', axis=0, tiled=True)  176 us
    all_gather x1, waiting for transfers between devices, per_device(): lax.all_gather(in_weight[0], 'fsdp', axis=0, tiled=True)  117 us
    dot_general x6, matrix products, contract_rows(): lax.dot_general(left, right, (((0,), (0,)), ((), ())), preferred_element_...  116 us
    dot_general x12, matrix products, state_space(): jnp.einsum('skijh,skjhp->skihp', weighted, values_k, precision=highest)  93.3 us
    psum x1, waiting for transfers between devices, per_device(): small_total = lax.psum(small_acc, ('dp', 'fsdp'))  83.1 us
    dot_general x9, matrix products, contract_cols(): lax.dot_general(left, right, (((1,), (1,)), ((), ())), preferred_element_...  67 us
    dot_general x12, matrix products, state_space(): jnp.einsum('skjhp,skjn->skhpn', scaled_values, in_k, precision=highest)  65.5 us
  transfers between devices with their start and end apart: 11, of which 10 were waited for; matrix products, arithmetic and copies ran while one was open for 18% of the time, Pallas kernels for 0%

commit v1 on v0

--- a/solution.py
+++ b/solution.py
@@ -13,6 +13,12 @@
 MICRO = 2
 epsilon = 1e-05
 highest = lax.Precision.HIGHEST
+
+
+def gather_from_all(x, axis, dim):
+    size = lax.axis_size(axis)
+    repeats = [size if d == dim else 1 for d in range(x.ndim)]
+    return lax.all_to_all(jnp.tile(x, repeats), axis, split_axis=dim, concat_axis=dim, tiled=True)
 
 
 def passed_along(block, axis, distance):
@@ -227,7 +233,7 @@
         total_in = part_in if total_in is None else total_in + part_in
         total_out = part_out if total_out is None else total_out + part_out
     owned_in, owned_out = (
-        lax.all_gather(total_in, "dp", axis=0, tiled=True),
+        gather_from_all(total_in, "dp", 0),
         lax.all_gather(total_out, "dp", axis=0, tiled=True),
     )
     small_total = lax.psum(small_acc, ("dp", "fsdp"))

time: 1790 us -> 1900 us (1.061)
  waiting for transfers between devices: 865 us -> 966 us
    reduce_scatter x1, waiting for transfers between devices: 0.98 us -> 338 us  [per_device(): lax.psum_scatter(column_term(mixed_cols, grad_rounded), ('dp', 'fsdp'), s...]
    all_gather x1 -> x0, waiting for transfers between devices: 176 us -> none  [per_device(): lax.all_gather(total_in, 'dp', axis=0, tiled=True)]
    reduce_scatter x1, waiting for transfers between devices: 391 us -> 322 us  [per_device(): lax.psum_scatter(column_term(normed_cols, grad_cat), ('dp', 'fsdp'), scat...]
    unnamed x603 -> x561, local copies, waits for them, and re-layouts: 48.6 us -> 45.7 us
  transfers between devices with their start and end apart: 11 -> 11, of which waited for: 10 -> 9; matrix products, arithmetic and copies ran while one was open for 18% -> 12% of each run, Pallas kernels for 0% -> 0%
where the time goes in v1:
time: 1900 us
  waiting for transfers between devices  966 us (51%)
  matrix products  463 us (24%)
  local copies, waits for them, and re-layouts  291 us (15%)
  other arithmetic  133 us (7%)
    reduce_scatter x1, waiting for transfers between devices, per_device(): lax.psum_scatter(column_term(mixed_cols, grad_rounded), ('dp', 'fsdp'), s...  338 us
    reduce_scatter x1, waiting for transfers between devices, per_device(): lax.psum_scatter(column_term(normed_cols, grad_cat), ('dp', 'fsdp'), scat...  322 us
    dot_general x6, matrix products, contract_rows(): lax.dot_general(left, right, (((0,), (0,)), ((), ())), preferred_element_...  125 us
    all_gather x1, waiting for transfers between devices, per_device(): lax.all_gather(in_weight[0], 'fsdp', axis=0, tiled=True)  118 us
    dot_general x12, matrix products, state_space(): jnp.einsum('skijh,skjhp->skihp', weighted, values_k, precision=highest)  92.9 us
    psum x1, waiting for transfers between devices, per_device(): small_total = lax.psum(small_acc, ('dp', 'fsdp'))  83.2 us
    dot_general x12, matrix products, state_space(): jnp.einsum('skjhp,skjn->skhpn', scaled_values, in_k, precision=highest)  67.5 us
    dot_general x9, matrix products, contract_cols(): lax.dot_general(left, right, (((1,), (1,)), ((), ())), preferred_element_...  67 us
  transfers between devices with their start and end apart: 11, of which 9 were waited for; matrix products, arithmetic and copies ran while one was open for 12% of the time, Pallas kernels for 0%

profile of v1, /device:TPU:0, one launch (start us, length us, event | category | flops | bytes accessed | tf_op | source)
XLA Modules:
  0.0 1895.3 jit_solution(7511097051946224348)
XLA Ops:
  8.9 6.6 all-gather.1
  18.9 117.8 %all-gather.9.cloned.1.call-done = bf16[1,1536,6400]{2,1,0:T(8,128)(2,1)} async-done(((bf16[1,384,6400]{2,1,0:T(8,128)(2,1)}), bf16[1,1536,6400]{2,1,0:T(8,128)(2,1)}) %all-gather.9.cloned.1.call-update) | async-done | bytes 19660816 | tf_op jit(solution)/shard_map/all_gather | solution.py:144
  136.7 8.1 fusion.10
  163.2 6.0 fusion.113
  183.9 18.6 all-gather.11.cloned.1.call-done
  214.0 14.2 collective-permute-done
  231.8 8.2 fusion.8
  267.5 6.0 fusion.103
  318.8 8.4 fusion.6
  337.5 5.9 fusion.204
  355.5 6.9 fusion.165
  367.7 8.0 bitcast_add_fusion.5
  385.8 9.2 fusion.241
  418.5 6.0 fusion.93
  436.2 7.5 multiply_reduce_fusion.20
  461.2 10.0 fusion.225
  495.5 7.4 fusion.329
  513.5 6.9 fusion.171
  526.3 7.9 bitcast_add_fusion.3
  538.9 6.6 bitcast_add_fusion.4
  567.8 13.8 fusion.4
  586.5 15.6 fusion.213
  631.1 7.9 fusion.240
  654.3 5.7 fusion.174
  662.8 10.7 fusion.227
  699.8 8.2 fusion.344
  712.5 6.8 fusion.177
  725.2 7.6 bitcast_add_fusion.1
  739.9 7.7 bitcast_add_fusion.2
  756.0 6.3 fusion.354
  772.8 14.3 fusion.2
  792.4 17.8 fusion.217
  841.5 5.9 fusion.359
  854.6 5.8 fusion.25
  860.5 6.0 bitcast_add_fusion
  876.3 10.4 fusion.229
  912.9 40.1 %add_add_fusion = f32[1536,6448]{1,0:T(8,128)} fusion(f32[1536,6448]{1,0:T(8,128)} %fusion.213, f32[1536,6448]{1,0:T(8,128)} %fusion.217, bf16[128,1536]{0,1:T(8,128)(2,1)S(1)} %bitcast.995, bf16[128,48]{1,0:T(8,128)(2,1)S(1)} %bitcast.1059, bf16[128,6400]{1,0:T(8,128)(2,1)S(1)} %fusion.232), kind=kOutput, calls=%fused_computation | convolution fusion | flops 2558566400 | bytes 120893440 | tf_op jit(solution)/shard_map/dot_general | solution.py:106
  956.7 11.3 fusion.396
  978.9 11.8 fusion.404
  990.6 28.6 %add_add_fusion.1 = f32[3072,1536]{1,0:T(8,128)} fusion(f32[3072,1536]{1,0:T(8,128)} %fusion.396, f32[3072,1536]{1,0:T(8,128)} %fusion.404, bf16[128,3072]{0,1:T(8,128)(2,1)} %bitcast.976, f32[128,1536]{1,0:T(8,128)} %collective-permute-done.3, pred[]{:T(512)S(6)} %eq.9), kind=kOutput, calls=%fused_computation.13 | convolution fusion | flops 1217593344 | bytes 58195968 | tf_op jit(solution)/shard_map/dot_general | solution.py:106
  1019.3 321.8 %reduce-scatter.3.cloned.1.call-done = f32[96,6448]{1,0:T(8,128)} async-done(((f32[1536,6448]{1,0:T(8,128)}), f32[96,6448]{1,0:T(8,128)}) %reduce-scatter.3.cloned.1.call-update) | async-done | bytes 2476048 | tf_op jit(solution)/shard_map/reduce_scatter | solution.py:227
  1341.1 6.1 tile.2
  1347.2 6.2 all-to-all-start
  1353.5 338.0 %reduce-scatter.5.cloned.1.call-done = f32[192,1536]{1,0:T(8,128)} async-done(((f32[3072,1536]{1,0:T(8,128)}), f32[192,1536]{1,0:T(8,128)}) %reduce-scatter.5.cloned.1.call-update) | async-done | bytes 1179664 | tf_op jit(solution)/shard_map/reduce_scatter | solution.py:230
  1701.4 10.9 fusion
  1720.4 61.0 %all-gather.7.cloned.1.call-done = f32[768,1536]{1,0:T(8,128)} async-done(((f32[192,1536]{1,0:T(8,128)}), f32[768,1536]{1,0:T(8,128)}) %all-gather.7.cloned.1.call-update) | async-done | bytes 4718608 | tf_op jit(solution)/shard_map/all_gather | solution.py:237
  1781.4 8.3 slice_bitcast_fusion
  1791.4 83.2 %all-reduce.63.cloned.1.call-done = (f32[1,1536]{1,0:T(1,128)}, f32[1,4,3328]{2,1,0:T(4,128)}, f32[1,3328]{1,0:T(1,128)}, f32[1,48]{1,0:T(1,128)}, f32[1,48]{1,0...) async-done(((f32[1,1536]{1,0:T(1,128)}, f32[1,4,3328]{2,1,0:T(4,128)}, f32[1,3328]{1,0:T(1,128)}, f32[1,48]{1,0:T(1,128)}, f32[1,48]{1,0:T(1,128)}, ...) | async-done | bytes 85584 | tf_op jit(solution)/shard_map/psum | solution.py:239
  (883 shorter events, 523.4 us)
Async XLA Ops:
  7.2 129.5 %all-gather.9.cloned.1.call-start = ((), (), s32[]{:S(2)}) async-start(), calls=%async_computation.4 | async-start | bytes 24576000 | tf_op jit(solution)/shard_map/all_gather | solution.py:144
  8.0 194.5 %all-gather.11.cloned.1.call-start = ((), (), s32[]{:S(2)}) async-start(), calls=%async_computation.5 | async-start | bytes 11796480 | tf_op jit(solution)/shard_map/all_gather | solution.py:146
  8.7 1332.4 %reduce-scatter.3.cloned.1.call-start = ((), (), s32[]{:S(2)}) async-start(), calls=%async_computation.6 | async-start | bytes 42614784 | tf_op jit(solution)/shard_map/reduce_scatter | solution.py:227
  8.8 221.0 %copy-start.135 = (f32[1536]{0:T(1024)}, f32[1536]{0:T(1024)S(1)}, u32[]{:S(2)}) copy-start(f32[1536]{0:T(1024)S(1)} %reduce.80) | copy-start | bytes 18436
  8.9 231.3 %copy-start.200 = (f32[3328]{0:T(1024)}, f32[3328]{0:T(1024)S(1)}, u32[]{:S(2)}) copy-start(f32[3328]{0:T(1024)S(1)} %reduce.78) | copy-start | bytes 39940
  15.5 771.6 %copy-start.78 = (bf16[1,1536,48]{1,2,0:T(8,128)(2,1)}, bf16[1,1536,48]{1,2,0:T(8,128)(2,1)S(1)}, u32[]{:S(2)}) copy-start(bf16[1,1536,48]{1,2,0:T(8,128)(2,1)S(1)} %all-gather.1) | copy-start | bytes 442372
  15.7 214.2 %copy-start.244 = (f32[128]{0:T(128)}, f32[128]{0:T(128)S(1)}, u32[]{:S(2)}) copy-start(f32[128]{0:T(128)S(1)} %add_rsqrt_fusion.5) | copy-start | bytes 1540
  15.7 284.7 %copy-start.237 = (f32[48]{0:T(128)}, f32[48]{0:T(128)S(1)}, u32[]{:S(2)}) copy-start(f32[48]{0:T(128)S(1)} %bitcast_negate_fusion) | copy-start | bytes 580
  18.6 266.6 %copy-start.127 = (f32[3072]{0:T(1024)}, f32[3072]{0:T(1024)S(1)}, u32[]{:S(2)}) copy-start(f32[3072]{0:T(1024)S(1)} %mul.1954) | copy-start | bytes 36868
  18.7 247.2 %copy-start.184 = (pred[64,64]{1,0:T(8,128)(4,1)}, pred[64,64]{1,0:T(8,128)(4,1)S(1)}, u32[]{:S(2)}) copy-start(pred[64,64]{1,0:T(8,128)(4,1)S(1)} %iota_compare_fusion) | copy-start | bytes 12292
  18.8 221.4 %copy-start.140 = (f32[3328]{0:T(1024)}, f32[3328]{0:T(1024)S(1)}, u32[]{:S(2)}) copy-start(f32[3328]{0:T(1024)S(1)} %get-tuple-element.99) | copy-start | bytes 39940
  18.8 221.4 %copy-start.145 = (f32[3328]{0:T(1024)}, f32[3328]{0:T(1024)S(1)}, u32[]{:S(2)}) copy-start(f32[3328]{0:T(1024)S(1)} %get-tuple-element.100) | copy-start | bytes 39940
  18.8 221.4 %copy-start.150 = (f32[3328]{0:T(1024)}, f32[3328]{0:T(1024)S(1)}, u32[]{:S(2)}) copy-start(f32[3328]{0:T(1024)S(1)} %get-tuple-element.101) | copy-start | bytes 39940
  18.8 221.4 %copy-start.155 = (f32[3328]{0:T(1024)}, f32[3328]{0:T(1024)S(1)}, u32[]{:S(2)}) copy-start(f32[3328]{0:T(1024)S(1)} %get-tuple-element.102) | copy-start | bytes 39940
  180.9 21.6 %copy-start.105 = (f32[1,3072]{1,0:T(1,128)S(1)}, f32[1,3072]{1,0:T(1,128)}, u32[]{:S(2)}) copy-start(f32[1,3072]{1,0:T(1,128)} %param.25) | copy-start | bytes 36868
  183.8 104.3 %copy-start.8 = (f32[1,128,3072]{2,1,0:T(8,128)}, f32[1,128,3072]{2,1,0:T(8,128)S(1)}, u32[]{:S(2)}) copy-start(f32[1,128,3072]{2,1,0:T(8,128)S(1)} %get-tuple-element.169) | copy-start | bytes 4718596
  183.9 104.3 %copy-start.241 = (f32[128]{0:T(128)}, f32[128]{0:T(128)S(1)}, u32[]{:S(2)}) copy-start(f32[128]{0:T(128)S(1)} %add_rsqrt_fusion.4) | copy-start | bytes 1540
  207.6 22.1 %copy-start.101 = (f32[128,1536]{1,0:T(8,128)}, f32[128,1536]{1,0:T(8,128)S(1)}, u32[]{:S(2)}) copy-start(f32[128,1536]{1,0:T(8,128)S(1)} %fusion.150) | copy-start | bytes 2359300
  207.6 20.6 %collective-permute-start = (f32[128,1536]{1,0:T(8,128)S(1)}, f32[128,1536]{1,0:T(8,128)S(1)}, u32[]{:S(2)}, u32[]{:S(2)}) collective-permute-start(f32[128,1536]{1,0:T(8,128)S(1)} %fusion.150), channel_id=1, source_target_pairs={{0,16},{1,17},{2,18},{3,19},{4,20},{5,21},{6,22},{7,23},{8,24},{9,... | collective-permute-start | bytes 2359304 | tf_op jit(solution)/shard_map/ppermute | solution.py:27
  231.8 68.7 %copy-start.119 = (f32[128,48]{1,0:T(8,128)}, f32[128,48]{1,0:T(8,128)S(1)}, u32[]{:S(2)}) copy-start(f32[128,48]{1,0:T(8,128)S(1)} %get-tuple-element.242) | copy-start | bytes 73732
  295.0 22.8 %copy-start.80 = (f32[128,1536]{1,0:T(8,128)}, f32[128,1536]{1,0:T(8,128)S(1)}, u32[]{:S(2)}) copy-start(f32[128,1536]{1,0:T(8,128)S(1)} %fusion.153) | copy-start | bytes 2359300
  295.0 20.9 %copy-start.40 = (f32[128,1536]{1,0:T(8,128)S(1)}, f32[128,1536]{1,0:T(8,128)}, u32[]{:S(2)}) copy-start(f32[128,1536]{1,0:T(8,128)} %copy-done.38) | copy-start | bytes 2359300
  295.0 20.9 %collective-permute-start.1 = (f32[128,1536]{1,0:T(8,128)S(1)}, f32[128,1536]{1,0:T(8,128)}, u32[]{:S(2)}, u32[]{:S(2)}) collective-permute-start(f32[128,1536]{1,0:T(8,128)S(1)} %fusion.153), channel_id=1, source_target_pairs={{0,16},{1,17},{2,18},{3,19},{4,20},{5,21},{6,22},{7,23},{8,24},{9,... | collective-permute-start | bytes 2359304 | tf_op jit(solution)/shard_map/ppermute | solution.py:27
  318.8 28.2 %copy-start.96 = (bf16[128,1536]{1,0:T(8,128)(2,1)}, bf16[128,1536]{1,0:T(8,128)(2,1)S(1)}, u32[]{:S(2)}) copy-start(bf16[128,1536]{1,0:T(8,128)(2,1)S(1)} %get-tuple-element.115) | copy-start | bytes 1179652
  345.7 108.1 %copy-start.110 = (f32[1,128,128]{2,1,0:T(8,128)}, f32[1,128,128]{2,1,0:T(8,128)S(1)}, u32[]{:S(2)}) copy-start(f32[1,128,128]{2,1,0:T(8,128)S(1)} %get-tuple-element.201) | copy-start | bytes 196612
  351.2 109.7 %copy-start.2 = (f32[2,64,48,64]{3,2,1,0:T(8,128)}, f32[2,64,48,64]{3,2,1,0:T(8,128)S(1)}, u32[]{:S(2)}) copy-start(f32[2,64,48,64]{3,2,1,0:T(8,128)S(1)} %reshape.2338) | copy-start | bytes 4718596
  505.8 122.0 %copy-start.106 = (f32[1,128,128]{2,1,0:T(8,128)}, f32[1,128,128]{2,1,0:T(8,128)S(1)}, u32[]{:S(2)}) copy-start(f32[1,128,128]{2,1,0:T(8,128)S(1)} %get-tuple-element.189) | copy-start | bytes 196612
  508.0 16.2 copy-start
  567.8 13.9 copy-start.82
  567.8 13.9 copy-start.137
  585.2 44.3 %collective-permute-start.2 = (f32[128,1536]{1,0:T(8,128)}, f32[128,1536]{1,0:T(8,128)}, u32[]{:S(2)}, u32[]{:S(2)}) collective-permute-start(f32[128,1536]{1,0:T(8,128)} %fusion.374), channel_id=1, source_target_pairs={{16,0},{17,1},{18,2},{19,3},{20,4},{21,5},{22,6},{23,7},{24,8},{25... | collective-permute-start | bytes 2359304 | tf_op jit(solution)/shard_map/ppermute | solution.py:27
  586.5 15.7 copy-start.35
  586.5 15.7 copy-start.97
  586.5 15.7 copy-start.245
  586.5 16.6 copy-start.28
  772.8 14.3 copy-start.138
  772.8 14.3 copy-start.249
  791.1 24.4 %collective-permute-start.3 = (f32[128,1536]{1,0:T(8,128)}, f32[128,1536]{1,0:T(8,128)}, u32[]{:S(2)}, u32[]{:S(2)}) collective-permute-start(f32[128,1536]{1,0:T(8,128)} %get-tuple-element.134), channel_id=1, source_target_pairs={{16,0},{17,1},{18,2},{19,3},{20,4},{21,5},{22,6},{23,7},{24,8},{25... | collective-permute-start | bytes 2359304 | tf_op jit(solution)/shard_map/ppermute | solution.py:27
  792.4 23.1 %slice-start = ((s8[9437184]{0:T(1024)(128)(4,1)}), s8[4194304]{0:T(1024)(128)(4,1)S(1)}, s32[]{:S(2)}) async-start(s8[9437184]{0:T(1024)(128)(4,1)} %bitcast.962), calls=%async_computation.9 | async-start | bytes 8388608
  792.4 23.1 %slice-start.1 = ((s8[9437184]{0:T(1024)(128)(4,1)}), s8[4194304]{0:T(1024)(128)(4,1)S(1)}, s32[]{:S(2)}) async-start(s8[9437184]{0:T(1024)(128)(4,1)} %bitcast.962), calls=%async_computation.10 | async-start | bytes 8388608
  792.4 23.1 %slice-start.2 = ((s8[9437184]{0:T(1024)(128)(4,1)}), s8[1048576]{0:T(1024)(128)(4,1)S(1)}, s32[]{:S(2)}) async-start(s8[9437184]{0:T(1024)(128)(4,1)} %bitcast.962), calls=%async_computation.11 | async-start | bytes 2097152
  876.3 14.6 copy-start.195
  876.3 14.8 copy-start.85
  953.0 738.4 %reduce-scatter.5.cloned.1.call-start = ((), (), s32[]{:S(2)}) async-start(), calls=%async_computation.7 | async-start | bytes 20054016 | tf_op jit(solution)/shard_map/reduce_scatter | solution.py:230
  1347.2 434.2 %all-to-all-start = ((f32[4,96,6448]{2,1,0:T(8,128)}), f32[4,96,6448]{2,1,0:T(8,128)}, u32[]{:S(2)}, u32[]{:S(2)}) async-start(f32[4,96,6448]{2,1,0:T(8,128)} %tile.2), calls=%async_computation | async-start | bytes 20054016 | tf_op jit(solution)/shard_map/all_to_all | solution.py:21
  1353.4 338.2 %copy-start.81 = (f32[128,1536]{1,0:T(8,128)S(1)}, f32[128,1536]{1,0:T(8,128)}, u32[]{:S(2)}) copy-start(f32[128,1536]{1,0:T(8,128)} %copy-done.80) | copy-start | bytes 2359300
  1353.4 428.0 %all-gather.7.cloned.1.call-start = ((), (), s32[]{:S(2)}) async-start(), calls=%async_computation.3 | async-start | bytes 5898240 | tf_op jit(solution)/shard_map/all_gather | solution.py:237
  1691.5 183.0 %all-reduce.63.cloned.1.call-start = ((), (), s32[]{:S(2)}) async-start(), calls=%async_computation.8 | async-start | bytes 173056 | tf_op jit(solution)/shard_map/psum | solution.py:239
  (239 other events, 989.3 us)
Sparse Core Ops, SparseCore 0:
  9.6 127.0 all-gather.8
  138.2 64.2 all-gather.10
  953.1 387.9 reduce-scatter.2
  1345.1 346.3 reduce-scatter.4
  1692.9 88.4 all-gather.6
  1786.8 87.7 all-reduce.62
